TPU v7x, 512 devices: a whole 4x8x8 slice. The times are simulated.
512 devices in a mesh: space: 64 (over z_lo, x, y), tm: 8 (over z_hi, core).
Axes of the slice: x: 4, y: 8, z: 8 (z_hi: 4, z_lo: 2; z = z_hi * 2 + z_lo), core: 2. Of those that a mesh axis runs over, the one named last changes fastest.
Arguments:
- source: bfloat16 [16, 128, 4, 2, 3, 16, 128], P('tm', 'space'), may hold values from -6 to 6
- gauge_links: bfloat16 [16, 128, 4, 2, 3, 3, 128], P('tm', 'space'), may hold values from -2.5 to 2.5
- clover: bfloat16 [16, 128, 2, 2, 6, 6, 128], P('tm', 'space'), may hold values from -0.3984375 to 0.3984375
- eigenvectors: bfloat16 [16, 128, 2, 3, 256, 128], P('tm', 'space'), may hold values from -4 to 4
- elemental: bfloat16 [16, 2, 256, 256], P('tm'), may hold values from -0.25 to 0.25
Outputs:
- sink_field: bfloat16 [16, 128, 4, 2, 3, 16, 128], P('tm', 'space')
All inputs are finite; a program needn't handle non-finite values.
Results may differ from a plain program's by a relative error of at most 0.0057.
Values may be sent and summed in bfloat16 or wider, within the bound.
No kernel may reach another device: no remote copies, remote signals or barrier semaphores. Data moves between devices by JAX's collectives and lax.ppermute only.
A program may use at most 64 MiB of HBM per device.

v0:
```python
import jax
import jax.numpy as jnp
from jax import lax
from jax.sharding import PartitionSpec as P

X = 16
Y = 8
HOPPING = 0.125
HALF_MAP = (
    ((1, 0.0, -1.0), (0, 0.0, -1.0)),
    ((1, -1.0, 0.0), (0, 1.0, 0.0)),
    ((0, 0.0, -1.0), (1, 0.0, 1.0)),
    ((0, 1.0, 0.0), (1, 1.0, 0.0)),
)


def passed_along(value, axis, by):
    count = lax.axis_size(axis)
    return lax.ppermute(value, axis, [(i, (i + by) % count) for i in range(count)])


def extended(cells, sides, width):
    for axis, dim in sides:
        count = lax.axis_size(axis)
        head = lax.slice_in_dim(cells, 0, width, axis=dim)
        tail = lax.slice_in_dim(cells, cells.shape[dim] - width, cells.shape[dim], axis=dim)
        cells = jnp.concatenate(
            [
                lax.ppermute(tail, axis, [(i, (i + 1) % count) for i in range(count)]),
                cells,
                lax.ppermute(head, axis, [((i + 1) % count, i) for i in range(count)]),
            ],
            axis=dim,
        )
    return cells


def dagger_map(forward_map):
    result = [None, None]
    for row_number in range(2):
        column, real_coef, imag_coef = forward_map[row_number]
        result[column] = (row_number, real_coef, -imag_coef)
    return tuple(result)


def apply_half(spin_map, half_spinor):
    outputs = []
    for column, real_coef, imag_coef in spin_map:
        picked = half_spinor[:, :, column]
        real_in = picked[:, :, 0]
        imag_in = picked[:, :, 1]
        outputs.append(
            jnp.stack(
                [
                    real_coef * real_in - imag_coef * imag_in,
                    real_coef * imag_in + imag_coef * real_in,
                ],
                axis=2,
            )
        )
    return jnp.stack(outputs, axis=2)


def project(spinor, spin_map, sign_value):
    return spinor[:, :, 0:2] + sign_value * apply_half(spin_map, spinor[:, :, 2:4])


def colour_apply(matrix, spinor):
    real_out = 0.0
    imag_out = 0.0
    for colour in range(3):
        left_real = matrix[:, :, 0, :, colour][:, :, None, :, None, :]
        left_imag = matrix[:, :, 1, :, colour][:, :, None, :, None, :]
        right_real = spinor[:, :, :, 0, colour][:, :, :, None]
        right_imag = spinor[:, :, :, 1, colour][:, :, :, None]
        real_out = real_out + left_real * right_real - left_imag * right_imag
        imag_out = imag_out + left_real * right_imag + left_imag * right_real
    return jnp.stack([real_out, imag_out], axis=3)


def adjoint(matrix):
    return jnp.stack(
        [jnp.swapaxes(matrix[:, :, 0], 2, 3), -jnp.swapaxes(matrix[:, :, 1], 2, 3)], axis=2
    )


def clover_apply(clover, spinor):
    block_list = []
    for chiral in range(2):
        clover_block = clover[:, :, chiral]
        new_shape = clover_block.shape[:2] + (2, 3, 6, clover_block.shape[-1])
        rows_real = clover_block[:, :, 0].reshape(new_shape)
        rows_imag = clover_block[:, :, 1].reshape(new_shape)
        real_out = 0.0
        imag_out = 0.0
        for source_index in range(6):
            spin_in = 2 * chiral + source_index // 3
            colour_in = source_index % 3
            left_real = rows_real[:, :, :, :, source_index][:, :, :, :, None, :]
            left_imag = rows_imag[:, :, :, :, source_index][:, :, :, :, None, :]
            right_real = spinor[:, :, spin_in, 0, colour_in][:, :, None, None]
            right_imag = spinor[:, :, spin_in, 1, colour_in][:, :, None, None]
            real_out = real_out + left_real * right_real - left_imag * right_imag
            imag_out = imag_out + left_real * right_imag + left_imag * right_real
        block_list.append(jnp.stack([real_out, imag_out], axis=3))
    return jnp.concatenate(block_list, axis=2)


def roll_plane(array_in, offset, hop_direction):
    sites = array_in.shape[-1]
    period = X if hop_direction == 0 else Y
    stride = 1 if hop_direction == 0 else X
    position = jnp.arange(sites) // stride % period
    if offset < 0:
        at_edge = position == period - 1
        wrapped = jnp.roll(array_in, (period - 1) * stride, axis=-1)
        plain = jnp.roll(array_in, -stride, axis=-1)
    else:
        at_edge = position == 0
        wrapped = jnp.roll(array_in, -(period - 1) * stride, axis=-1)
        plain = jnp.roll(array_in, stride, axis=-1)
    return jnp.where(at_edge, wrapped, plain)


def dirac_region(padded, centre_links, back_z, back_t, clover):
    centre = padded[1:-1, 1:-1]
    hopping = 0.0
    for hop_direction in range(4):
        forward_map = HALF_MAP[hop_direction]
        backward_map = dagger_map(forward_map)
        here_links = centre_links[:, :, hop_direction]
        if hop_direction < 2:
            ahead = roll_plane(project(centre, forward_map, -1.0), -1, hop_direction)
            behind = roll_plane(
                colour_apply(adjoint(here_links), project(centre, forward_map, 1.0)),
                1,
                hop_direction,
            )
        else:
            if hop_direction == 2:
                ahead_full = padded[1:-1, 2:]
                behind_full = padded[1:-1, :-2]
                behind_links = back_z
            else:
                ahead_full = padded[2:, 1:-1]
                behind_full = padded[:-2, 1:-1]
                behind_links = back_t
            ahead = project(ahead_full, forward_map, -1.0)
            behind = colour_apply(adjoint(behind_links), project(behind_full, forward_map, 1.0))
        forward_part = colour_apply(here_links, ahead)
        hopping = hopping + jnp.concatenate(
            [forward_part + behind, apply_half(backward_map, behind - forward_part)], axis=2
        )
    return centre + clover_apply(clover, centre) - HOPPING * hopping


def reverse_time(padded, depth_rows, position, tm_count):
    slices = padded.shape[0]
    slice_ids = jnp.arange(slices)
    negate = jnp.logical_or(
        jnp.logical_and(slice_ids < depth_rows, position == 0),
        jnp.logical_and(slice_ids >= slices - depth_rows, position == tm_count - 1),
    )
    factor = jnp.where(negate, -1.0, 1.0).astype(jnp.float32)
    return padded * factor.reshape((slices,) + (1,) * (padded.ndim - 1))


def mix_coefficients(elemental, coefficients):
    slices = coefficients.shape[0]
    eigen_count = coefficients.shape[1]
    complex_pairs = coefficients.reshape(slices, eigen_count, -1, 2)
    elemental_f32 = elemental.astype(jnp.float32)

    def product(left_factor, right_factor):
        return jnp.einsum(
            "ogs,osq->ogq", left_factor, right_factor, precision=lax.Precision.HIGHEST
        )

    mixed_real = product(elemental_f32[:, 0], complex_pairs[..., 0]) - product(
        elemental_f32[:, 1], complex_pairs[..., 1]
    )
    mixed_imag = product(elemental_f32[:, 0], complex_pairs[..., 1]) + product(
        elemental_f32[:, 1], complex_pairs[..., 0]
    )
    return (
        jnp.stack([mixed_real, mixed_imag], axis=-1)
        .reshape(slices, eigen_count, -1)
        .astype(jnp.bfloat16)
    )


def on_device(source, gauge_links, clover, eigenvectors, elemental):
    slices = source.shape[0]
    layers = source.shape[1]
    column_list = source.shape[5]
    eigen_count = eigenvectors.shape[4]
    tm_position = lax.axis_index("tm")
    tm_count = lax.axis_size("tm")
    links_f32 = gauge_links.astype(jnp.float32)
    clover_f32 = clover.astype(jnp.float32)
    edge_z = passed_along(gauge_links[:, -1:, 2], "space", 1)
    edge_t = passed_along(gauge_links[-1:, :, 3], "tm", 1)
    back_z = jnp.concatenate([edge_z, gauge_links[:, :-1, 2]], axis=1).astype(jnp.float32)
    back_t = jnp.concatenate([edge_t, gauge_links[:-1, :, 3]], axis=0).astype(jnp.float32)

    def apply_once(spinor_in):
        padded = extended(spinor_in, (("space", 1), ("tm", 0)), 1)
        padded = reverse_time(padded, 1, tm_position, tm_count)
        return dirac_region(padded, links_f32, back_z, back_t, clover_f32)

    def apply_twice(spinor_in):
        return apply_once(apply_once(spinor_in))

    forward = apply_twice(source.astype(jnp.float32))
    rounded = forward.astype(jnp.bfloat16)
    normaliser = (3.0 * X * Y * layers * lax.axis_size("space")) ** (-0.5)
    products = 0.0
    for colour in range(3):
        products = products + lax.dot_general(
            eigenvectors[:, :, :, colour],
            rounded[:, :, :, :, colour],
            (((1, 4), (1, 5)), ((0,), (0,))),
            preferred_element_type=jnp.float32,
        )
    real_part = products[:, 0, :, :, 0] + products[:, 1, :, :, 1]
    imag_part = products[:, 0, :, :, 1] - products[:, 1, :, :, 0]
    partial_sums = (
        jnp.stack([real_part, imag_part], axis=-1).reshape(slices, eigen_count, 8 * column_list)
        * normaliser
    )
    share_sums = lax.psum_scatter(partial_sums, "space", scatter_dimension=2, tiled=True)
    mixed_coef = lax.all_gather(
        mix_coefficients(elemental, share_sums), "space", axis=2, tiled=True
    )
    complex_pairs = mixed_coef.reshape(slices, eigen_count, 4, column_list, 2)
    mixed_real = complex_pairs[..., 0]
    mixed_imag = complex_pairs[..., 1]
    first_row = jnp.stack([mixed_real, mixed_imag], axis=3)
    second_row = jnp.stack([-mixed_imag, mixed_real], axis=3)
    left_operand = jnp.stack([first_row, second_row], axis=1)
    colour_parts = [
        lax.dot_general(
            left_operand,
            eigenvectors[:, :, :, colour],
            (((1, 2), (2, 3)), ((0,), (0,))),
            preferred_element_type=jnp.float32,
        )
        for colour in range(3)
    ]
    expanded = jnp.moveaxis(jnp.stack(colour_parts, axis=3), 5, 1) * eigen_count ** (-0.5)
    return apply_twice(expanded).astype(jnp.bfloat16)


def solution(mesh):
    placed = (
        P("tm", "space", None, None, None, None, None),
        P("tm", "space", None, None, None, None, None),
        P("tm", "space", None, None, None, None, None),
        P("tm", "space", None, None, None, None),
        P("tm", None, None, None),
    )
    return jax.shard_map(
        on_device,
        mesh=mesh,
        in_specs=placed,
        out_specs=P("tm", "space", None, None, None, None, None),
        check_vma=False,
    )
```

profile of v0, /device:TPU:129, one launch (start us, length us, event | category | flops | bytes accessed | tf_op | source)
XLA Modules:
  0.0 963.1 jit_solution(2014216765966501170)
XLA Ops:
  6.5 1.1 copy_convert_fusion
  7.8 3.2 collective-permute-start
  11.0 7.8 collective-permute-start.1
  18.8 0.7 fusion.202
  19.6 7.0 collective-permute-start.5
  26.5 0.7 slice_bitcast_fusion.379
  27.3 0.6 copy.764
  27.9 1.9 collective-permute-start.4
  29.8 0.9 copy_convert_fusion.1
  31.5 0.6 broadcast_compare_fusion
  33.5 1.9 collective-permute-start.2
  35.4 2.4 collective-permute-start.3
  37.8 0.8 maximum_convert_fusion
  38.8 13.6 %collective-permute-done.2 = f32[1,4,4,2,3,16,128]{6,5,1,3,0,4,2:T(8,128)S(1)} collective-permute-done((f32[1,4,4,2,3,16,128]{6,5,1,3,0,4,2:T(8,128)S(1)}, f32[1,4,4,2,3,16,128]{6,5,1,3,0,4,2:T(8,128)S(1)}, u32[]{:S(2)}, u32[]{:S(2)}) %collective-permute-start.2) | collective-permute-done | bytes 786464 | tf_op jit(solution)/shard_map/ppermute | solution.py:29
  52.4 6.9 collective-permute-done.3
  67.2 1.9 collective-permute-start.6
  69.2 7.6 collective-permute-start.7
  76.7 4.4 collective-permute-done.6
  81.2 1.8 collective-permute-done.7
  83.0 1.3 fusion.193
  84.3 5.4 collective-permute-start.8
  89.7 2.1 collective-permute-start.9
  91.9 1.3 dynamic-slice
  93.8 1.5 fusion.192
  95.3 9.9 %collective-permute-done.8 = f32[1,4,4,2,3,16,128]{6,5,1,3,0,4,2:T(8,128)} collective-permute-done((f32[1,4,4,2,3,16,128]{6,5,1,3,0,4,2:T(8,128)}, f32[1,4,4,2,3,16,128]{6,5,1,3,0,4,2:T(8,128)}, u32[]{:S(2)}, u32[]{:S(2)}) %collective-permute-start.8) | collective-permute-done | bytes 786464 | tf_op jit(solution)/shard_map/ppermute | solution.py:29
  105.1 7.8 collective-permute-done.9
  113.0 1.8 maximum_multiply_fusion.1
  124.2 0.9 copy.796
  125.2 530.7 %all-reduce.3.cloned.1.call-done = f32[2,256,128]{1,0,2:T(2,128)} async-done(((f32[2,256,128]{1,0,2:T(2,128)}), f32[2,256,128]{1,0,2:T(2,128)}) %all-reduce.3.cloned.1.call-update) | async-done | bytes 262160
  655.9 0.7 dynamic-slice_bitcast_fusion
  657.9 125.5 %all-gather = bf16[2,256,1,128]{1,0,2,3:T(2,128)(2,1)S(1)} all-gather(bf16[2,256,1,2]{1,0,2,3:T(2,128)(2,1)S(1)} %pad_maximum_fusion.50), channel_id=2, replica_groups=mesh['space'=64,'tm'=8] {'space'}, dimensions={3}, use_global_device_ids=true | all-gather | bytes 133120 | tf_op jit(solution)/shard_map/all_gather | solution.py:232
  784.5 1.9 collective-permute-start.10
  786.4 7.6 collective-permute-start.11
  794.0 3.2 collective-permute-done.10
  797.2 1.5 collective-permute-done.11
  799.1 65.2 %collective-permute-start.12 = (f32[1,4,4,2,3,16,128]{6,5,1,3,0,4,2:T(8,128)S(1)}, f32[1,4,4,2,3,16,128]{6,5,1,3,0,4,2:T(8,128)S(1)}, u32[]{:S(2)}, u32[]{:S(2)}) collective-permute-start(f32[1,4,4,2,3,16,128]{6,5,1,3,0,4,2:T(8,128)S(1)} %get-tuple-element.180), channel_id=1, source_target_pairs={{0,1},{1,2},{2,3},{3,4},{4,5},{5,6},{6,7},{7,0},{8,9},{9,10},{10,1... | collective-permute-start | bytes 2359304 | tf_op jit(solution)/shard_map/ppermute | solution.py:29
  864.3 2.1 collective-permute-start.13
  866.4 15.2 %collective-permute-done.12 = f32[1,4,4,2,3,16,128]{6,5,1,3,0,4,2:T(8,128)S(1)} collective-permute-done((f32[1,4,4,2,3,16,128]{6,5,1,3,0,4,2:T(8,128)S(1)}, f32[1,4,4,2,3,16,128]{6,5,1,3,0,4,2:T(8,128)S(1)}, u32[]{:S(2)}, u32[]{:S(2)}) %collective-permute-start.12) | collective-permute-done | bytes 786464 | tf_op jit(solution)/shard_map/ppermute | solution.py:29
  881.6 6.5 collective-permute-done.13
  888.1 0.6 maximum_multiply_fusion.2
  897.3 1.9 collective-permute-start.14
  899.2 10.6 %collective-permute-start.15 = (f32[2,1,4,2,3,16,128]{6,5,1,3,2,0,4:T(8,128)S(1)}, f32[2,1,4,2,3,16,128]{6,5,1,3,2,0,4:T(8,128)S(1)}, u32[]{:S(2)}, u32[]{:S(2)}) collective-permute-start(f32[2,1,4,2,3,16,128]{6,5,1,3,2,0,4:T(8,128)S(1)} %get-tuple-element.212), channel_id=1, source_target_pairs={{8,0},{16,8},{24,16},{32,24},{40,32},{48,40},{56,48},{64,56},{72,6... | collective-permute-start | bytes 1179656 | tf_op jit(solution)/shard_map/ppermute | solution.py:31
  909.7 7.4 collective-permute-done.14
  917.5 7.5 collective-permute-start.16
  925.0 2.2 collective-permute-start.17
  927.2 10.9 %collective-permute-done.16 = f32[1,4,4,2,3,16,128]{6,5,1,3,2,0,4:T(8,128)S(1)} collective-permute-done((f32[1,4,4,2,3,16,128]{6,5,1,3,2,0,4:T(8,128)S(1)}, f32[1,4,4,2,3,16,128]{6,5,1,3,2,0,4:T(8,128)S(1)}, u32[]{:S(2)}, u32[]{:S(2)}) %collective-permute-start.16) | collective-permute-done | bytes 786464 | tf_op jit(solution)/shard_map/ppermute | solution.py:29
  938.1 9.4 collective-permute-done.17
  955.4 0.8 copy.863
  (620 shorter events, 35.4 us)
Async XLA Ops:
  6.5 25.7 %copy-start.103 = (bf16[2,2,2,2,6,6,128]{6,3,5,4,2,1,0:T(2,128)(2,1)S(1)}, bf16[2,2,2,2,6,6,128]{6,3,5,4,2,1,0:T(2,128)(2,1)}, u32[]{:S(2)}) copy-start(bf16[2,2,2,2,6,6,128]{6,3,5,4,2,1,0:T(2,128)(2,1)} %param.7) | copy-start | bytes 442372
  6.5 649.4 %all-reduce.3.cloned.1.call-start = ((), (), s32[]{:S(2)}) async-start(), calls=%async_computation | async-start | bytes 524288
  7.8 25.4 %collective-permute-start = (f32[2,1,4,2,3,16,128]{6,5,1,3,0,4,2:T(8,128)S(1)}, f32[2,1,4,2,3,16,128]{6,5,1,3,0,4,2:T(8,128)S(1)}, u32[]{:S(2)}, u32[]{:S(2)}) collective-permute-start(f32[2,1,4,2,3,16,128]{6,5,1,3,0,4,2:T(8,128)S(1)} %get-tuple-element.247), channel_id=1, source_target_pairs={{0,8},{8,16},{16,24},{24,32},{32,40},{40,48},{48,56},{56,64},{64,7... | collective-permute-start | bytes 1179656 | tf_op jit(solution)/shard_map/ppermute | solution.py:29
  11.0 22.2 %collective-permute-start.1 = (f32[2,1,4,2,3,16,128]{6,5,1,3,0,4,2:T(8,128)S(1)}, f32[2,1,4,2,3,16,128]{6,5,1,3,0,4,2:T(8,128)S(1)}, u32[]{:S(2)}, u32[]{:S(2)}) collective-permute-start(f32[2,1,4,2,3,16,128]{6,5,1,3,0,4,2:T(8,128)S(1)} %get-tuple-element.248), channel_id=1, source_target_pairs={{8,0},{16,8},{24,16},{32,24},{40,32},{48,40},{56,48},{64,56},{72,6... | collective-permute-start | bytes 1179656 | tf_op jit(solution)/shard_map/ppermute | solution.py:31
  19.6 13.6 %collective-permute-start.5 = (bf16[1,2,2,3,3,128]{5,1,4,3,2,0:T(2,128)(2,1)S(1)}, bf16[1,2,2,3,3,128]{5,1,4,3,2,0:T(2,128)(2,1)S(1)}, u32[]{:S(2)}, u32[]{:S(2)}) collective-permute-start(bf16[1,2,2,3,3,128]{5,1,4,3,2,0:T(2,128)(2,1)S(1)} %bitcast.1310), channel_id=1, source_target_pairs={{0,1},{1,2},{2,3},{3,4},{4,5},{5,6},{6,7},{7,0},{8,9},{9,10},{10,1... | collective-permute-start | bytes 27656 | tf_op jit(solution)/shard_map/ppermute | solution.py:19
  27.9 9.9 %collective-permute-start.4 = (bf16[2,1,2,3,3,128]{5,1,4,3,2,0:T(2,128)(2,1)}, bf16[2,1,2,3,3,128]{5,1,4,3,2,0:T(2,128)(2,1)}, u32[]{:S(2)}, u32[]{:S(2)}) collective-permute-start(bf16[2,1,2,3,3,128]{5,1,4,3,2,0:T(2,128)(2,1)} %copy.764), channel_id=1, source_target_pairs={{0,8},{8,16},{16,24},{24,32},{32,40},{40,48},{48,56},{56,64},{64,7... | collective-permute-start | bytes 27656 | tf_op jit(solution)/shard_map/ppermute | solution.py:19
  32.1 32.4 %copy-start.31 = (f32[2,2,3,128]{3,1,2,0:T(2,128)}, f32[2,2,3,128]{3,1,2,0:T(2,128)S(1)}, u32[]{:S(2)}) copy-start(f32[2,2,3,128]{3,1,2,0:T(2,128)S(1)} %get-tuple-element.761) | copy-start | bytes 18436
  32.1 32.4 %copy-start.34 = (f32[2,2,3,128]{3,1,2,0:T(2,128)}, f32[2,2,3,128]{3,1,2,0:T(2,128)S(1)}, u32[]{:S(2)}) copy-start(f32[2,2,3,128]{3,1,2,0:T(2,128)S(1)} %get-tuple-element.762) | copy-start | bytes 18436
  32.1 32.4 %copy-start.37 = (f32[2,2,3,128]{3,1,2,0:T(2,128)}, f32[2,2,3,128]{3,1,2,0:T(2,128)S(1)}, u32[]{:S(2)}) copy-start(f32[2,2,3,128]{3,1,2,0:T(2,128)S(1)} %get-tuple-element.763) | copy-start | bytes 18436
  32.1 32.4 %copy-start.40 = (f32[2,2,3,128]{3,1,2,0:T(2,128)}, f32[2,2,3,128]{3,1,2,0:T(2,128)S(1)}, u32[]{:S(2)}) copy-start(f32[2,2,3,128]{3,1,2,0:T(2,128)S(1)} %get-tuple-element.764) | copy-start | bytes 18436
  32.1 32.4 %copy-start.43 = (f32[2,2,3,128]{3,1,2,0:T(2,128)}, f32[2,2,3,128]{3,1,2,0:T(2,128)S(1)}, u32[]{:S(2)}) copy-start(f32[2,2,3,128]{3,1,2,0:T(2,128)S(1)} %get-tuple-element.765) | copy-start | bytes 18436
  32.1 32.4 %copy-start.46 = (f32[2,2,3,128]{3,1,2,0:T(2,128)}, f32[2,2,3,128]{3,1,2,0:T(2,128)S(1)}, u32[]{:S(2)}) copy-start(f32[2,2,3,128]{3,1,2,0:T(2,128)S(1)} %get-tuple-element.766) | copy-start | bytes 18436
  32.1 28.6 %copy-start.67 = (f32[2,2,3,128]{3,1,2,0:T(2,128)}, f32[2,2,3,128]{3,1,2,0:T(2,128)S(1)}, u32[]{:S(2)}) copy-start(f32[2,2,3,128]{3,1,2,0:T(2,128)S(1)} %get-tuple-element.767) | copy-start | bytes 18436
  32.2 28.6 %copy-start.70 = (f32[2,2,3,128]{3,1,2,0:T(2,128)}, f32[2,2,3,128]{3,1,2,0:T(2,128)S(1)}, u32[]{:S(2)}) copy-start(f32[2,2,3,128]{3,1,2,0:T(2,128)S(1)} %get-tuple-element.768) | copy-start | bytes 18436
  32.2 28.6 %copy-start.73 = (f32[2,2,3,128]{3,1,2,0:T(2,128)}, f32[2,2,3,128]{3,1,2,0:T(2,128)S(1)}, u32[]{:S(2)}) copy-start(f32[2,2,3,128]{3,1,2,0:T(2,128)S(1)} %get-tuple-element.769) | copy-start | bytes 18436
  32.2 28.6 %copy-start.76 = (f32[2,2,3,128]{3,1,2,0:T(2,128)}, f32[2,2,3,128]{3,1,2,0:T(2,128)S(1)}, u32[]{:S(2)}) copy-start(f32[2,2,3,128]{3,1,2,0:T(2,128)S(1)} %get-tuple-element.770) | copy-start | bytes 18436
  32.2 28.6 %copy-start.79 = (f32[2,2,3,128]{3,1,2,0:T(2,128)}, f32[2,2,3,128]{3,1,2,0:T(2,128)S(1)}, u32[]{:S(2)}) copy-start(f32[2,2,3,128]{3,1,2,0:T(2,128)S(1)} %get-tuple-element.771) | copy-start | bytes 18436
  32.2 28.6 %copy-start.82 = (f32[2,2,3,128]{3,1,2,0:T(2,128)}, f32[2,2,3,128]{3,1,2,0:T(2,128)S(1)}, u32[]{:S(2)}) copy-start(f32[2,2,3,128]{3,1,2,0:T(2,128)S(1)} %get-tuple-element.772) | copy-start | bytes 18436
  33.0 29.8 %copy-start.13 = (f32[2,2,3,128]{3,1,2,0:T(2,128)}, f32[2,2,3,128]{3,1,2,0:T(2,128)S(1)}, u32[]{:S(2)}) copy-start(f32[2,2,3,128]{3,1,2,0:T(2,128)S(1)} %get-tuple-element.717) | copy-start | bytes 18436
  33.0 29.8 %copy-start.16 = (f32[2,2,3,128]{3,1,2,0:T(2,128)}, f32[2,2,3,128]{3,1,2,0:T(2,128)S(1)}, u32[]{:S(2)}) copy-start(f32[2,2,3,128]{3,1,2,0:T(2,128)S(1)} %get-tuple-element.718) | copy-start | bytes 18436
  33.0 29.8 %copy-start.19 = (f32[2,2,3,128]{3,1,2,0:T(2,128)}, f32[2,2,3,128]{3,1,2,0:T(2,128)S(1)}, u32[]{:S(2)}) copy-start(f32[2,2,3,128]{3,1,2,0:T(2,128)S(1)} %get-tuple-element.719) | copy-start | bytes 18436
  33.0 29.8 %copy-start.22 = (f32[2,2,3,128]{3,1,2,0:T(2,128)}, f32[2,2,3,128]{3,1,2,0:T(2,128)S(1)}, u32[]{:S(2)}) copy-start(f32[2,2,3,128]{3,1,2,0:T(2,128)S(1)} %get-tuple-element.720) | copy-start | bytes 18436
  33.0 29.8 %copy-start.25 = (f32[2,2,3,128]{3,1,2,0:T(2,128)}, f32[2,2,3,128]{3,1,2,0:T(2,128)S(1)}, u32[]{:S(2)}) copy-start(f32[2,2,3,128]{3,1,2,0:T(2,128)S(1)} %get-tuple-element.721) | copy-start | bytes 18436
  33.0 29.8 %copy-start.28 = (f32[2,2,3,128]{3,1,2,0:T(2,128)}, f32[2,2,3,128]{3,1,2,0:T(2,128)S(1)}, u32[]{:S(2)}) copy-start(f32[2,2,3,128]{3,1,2,0:T(2,128)S(1)} %get-tuple-element.722) | copy-start | bytes 18436
  33.0 30.5 %copy-start.1 = (f32[2,2,3,128]{3,1,2,0:T(2,128)}, f32[2,2,3,128]{3,1,2,0:T(2,128)S(1)}, u32[]{:S(2)}) copy-start(f32[2,2,3,128]{3,1,2,0:T(2,128)S(1)} %get-tuple-element.795) | copy-start | bytes 18436
  33.1 30.5 %copy-start.4 = (f32[2,2,3,128]{3,1,2,0:T(2,128)}, f32[2,2,3,128]{3,1,2,0:T(2,128)S(1)}, u32[]{:S(2)}) copy-start(f32[2,2,3,128]{3,1,2,0:T(2,128)S(1)} %get-tuple-element.796) | copy-start | bytes 18436
  33.1 30.5 %copy-start.7 = (f32[2,2,3,128]{3,1,2,0:T(2,128)}, f32[2,2,3,128]{3,1,2,0:T(2,128)S(1)}, u32[]{:S(2)}) copy-start(f32[2,2,3,128]{3,1,2,0:T(2,128)S(1)} %get-tuple-element.797) | copy-start | bytes 18436
  33.1 30.5 %copy-start.10 = (f32[2,2,3,128]{3,1,2,0:T(2,128)}, f32[2,2,3,128]{3,1,2,0:T(2,128)S(1)}, u32[]{:S(2)}) copy-start(f32[2,2,3,128]{3,1,2,0:T(2,128)S(1)} %get-tuple-element.798) | copy-start | bytes 18436
  33.1 26.1 %copy-start.110 = (f32[4]{0:T(128)}, f32[4]{0:T(128)S(1)}, u32[]{:S(2)}) copy-start(f32[4]{0:T(128)S(1)} %or_select_fusion) | copy-start | bytes 52
  33.5 18.9 %collective-permute-start.2 = (f32[1,4,4,2,3,16,128]{6,5,1,3,0,4,2:T(8,128)S(1)}, f32[1,4,4,2,3,16,128]{6,5,1,3,0,4,2:T(8,128)S(1)}, u32[]{:S(2)}, u32[]{:S(2)}) collective-permute-start(f32[1,4,4,2,3,16,128]{6,5,1,3,0,4,2:T(8,128)S(1)} %get-tuple-element.187), channel_id=1, source_target_pairs={{0,1},{1,2},{2,3},{3,4},{4,5},{5,6},{6,7},{7,0},{8,9},{9,10},{10,1... | collective-permute-start | bytes 2359304 | tf_op jit(solution)/shard_map/ppermute | solution.py:29
  35.4 23.8 %collective-permute-start.3 = (f32[1,4,4,2,3,16,128]{6,5,1,3,0,4,2:T(8,128)S(1)}, f32[1,4,4,2,3,16,128]{6,5,1,3,0,4,2:T(8,128)S(1)}, u32[]{:S(2)}, u32[]{:S(2)}) collective-permute-start(f32[1,4,4,2,3,16,128]{6,5,1,3,0,4,2:T(8,128)S(1)} %get-tuple-element.188), channel_id=1, source_target_pairs={{1,0},{2,1},{3,2},{4,3},{5,4},{6,5},{7,6},{0,7},{9,8},{10,9},{11,1... | collective-permute-start | bytes 2359304 | tf_op jit(solution)/shard_map/ppermute | solution.py:31
  38.7 25.0 %copy-start.49 = (f32[2,2,3,128]{3,1,2,0:T(2,128)}, f32[2,2,3,128]{3,1,2,0:T(2,128)S(1)}, u32[]{:S(2)}) copy-start(f32[2,2,3,128]{3,1,2,0:T(2,128)S(1)} %get-tuple-element.758) | copy-start | bytes 18436
  38.7 25.0 %copy-start.52 = (f32[2,2,3,128]{3,1,2,0:T(2,128)}, f32[2,2,3,128]{3,1,2,0:T(2,128)S(1)}, u32[]{:S(2)}) copy-start(f32[2,2,3,128]{3,1,2,0:T(2,128)S(1)} %get-tuple-element.759) | copy-start | bytes 18436
  38.7 25.0 %copy-start.55 = (f32[2,2,3,128]{3,1,2,0:T(2,128)}, f32[2,2,3,128]{3,1,2,0:T(2,128)S(1)}, u32[]{:S(2)}) copy-start(f32[2,2,3,128]{3,1,2,0:T(2,128)S(1)} %get-tuple-element.760) | copy-start | bytes 18436
  67.2 14.0 %collective-permute-start.6 = (f32[2,1,4,2,3,16,128]{6,5,1,3,0,4,2:T(8,128)S(1)}, f32[2,1,4,2,3,16,128]{6,5,1,3,0,4,2:T(8,128)S(1)}, u32[]{:S(2)}, u32[]{:S(2)}) collective-permute-start(f32[2,1,4,2,3,16,128]{6,5,1,3,0,4,2:T(8,128)S(1)} %get-tuple-element.235), channel_id=1, source_target_pairs={{0,8},{8,16},{16,24},{24,32},{32,40},{40,48},{48,56},{56,64},{64,7... | collective-permute-start | bytes 1179656 | tf_op jit(solution)/shard_map/ppermute | solution.py:29
  69.2 13.8 %collective-permute-start.7 = (f32[2,1,4,2,3,16,128]{6,5,1,3,0,4,2:T(8,128)S(1)}, f32[2,1,4,2,3,16,128]{6,5,1,3,0,4,2:T(8,128)S(1)}, u32[]{:S(2)}, u32[]{:S(2)}) collective-permute-start(f32[2,1,4,2,3,16,128]{6,5,1,3,0,4,2:T(8,128)S(1)} %get-tuple-element.236), channel_id=1, source_target_pairs={{8,0},{16,8},{24,16},{32,24},{40,32},{48,40},{56,48},{64,56},{72,6... | collective-permute-start | bytes 1179656 | tf_op jit(solution)/shard_map/ppermute | solution.py:31
  84.3 20.8 %collective-permute-start.8 = (f32[1,4,4,2,3,16,128]{6,5,1,3,0,4,2:T(8,128)}, f32[1,4,4,2,3,16,128]{6,5,1,3,0,4,2:T(8,128)}, u32[]{:S(2)}, u32[]{:S(2)}) collective-permute-start(f32[1,4,4,2,3,16,128]{6,5,1,3,0,4,2:T(8,128)} %get-tuple-element.185), channel_id=1, source_target_pairs={{0,1},{1,2},{2,3},{3,4},{4,5},{5,6},{6,7},{7,0},{8,9},{9,10},{10,1... | collective-permute-start | bytes 2359304 | tf_op jit(solution)/shard_map/ppermute | solution.py:29
  89.7 23.2 %collective-permute-start.9 = (f32[1,4,4,2,3,16,128]{6,5,1,3,0,4,2:T(8,128)}, f32[1,4,4,2,3,16,128]{6,5,1,3,0,4,2:T(8,128)}, u32[]{:S(2)}, u32[]{:S(2)}) collective-permute-start(f32[1,4,4,2,3,16,128]{6,5,1,3,0,4,2:T(8,128)} %get-tuple-element.186), channel_id=1, source_target_pairs={{1,0},{2,1},{3,2},{4,3},{5,4},{6,5},{7,6},{0,7},{9,8},{10,9},{11,1... | collective-permute-start | bytes 2359304 | tf_op jit(solution)/shard_map/ppermute | solution.py:31
  123.8 532.8 %copy-start = (bf16[2,2,256,256]{3,2,1,0:T(8,128)(2,1)S(1)}, bf16[2,2,256,256]{3,2,1,0:T(8,128)(2,1)}, u32[]{:S(2)}) copy-start(bf16[2,2,256,256]{3,2,1,0:T(8,128)(2,1)} %param.9) | copy-start | bytes 1572868
  784.5 12.7 %collective-permute-start.10 = (f32[2,1,4,2,3,16,128]{6,5,1,3,0,4,2:T(8,128)S(1)}, f32[2,1,4,2,3,16,128]{6,5,1,3,0,4,2:T(8,128)S(1)}, u32[]{:S(2)}, u32[]{:S(2)}) collective-permute-start(f32[2,1,4,2,3,16,128]{6,5,1,3,0,4,2:T(8,128)S(1)} %get-tuple-element.223), channel_id=1, source_target_pairs={{0,8},{8,16},{16,24},{24,32},{32,40},{40,48},{48,56},{56,64},{64,7... | collective-permute-start | bytes 1179656 | tf_op jit(solution)/shard_map/ppermute | solution.py:29
  786.4 101.7 %copy-start.111 = (f32[4]{0:T(128)S(1)}, f32[4]{0:T(128)}, u32[]{:S(2)}) copy-start(f32[4]{0:T(128)} %copy-done.110) | copy-start | bytes 52
  786.4 12.3 %collective-permute-start.11 = (f32[2,1,4,2,3,16,128]{6,5,1,3,0,4,2:T(8,128)S(1)}, f32[2,1,4,2,3,16,128]{6,5,1,3,0,4,2:T(8,128)S(1)}, u32[]{:S(2)}, u32[]{:S(2)}) collective-permute-start(f32[2,1,4,2,3,16,128]{6,5,1,3,0,4,2:T(8,128)S(1)} %get-tuple-element.224), channel_id=1, source_target_pairs={{8,0},{16,8},{24,16},{32,24},{40,32},{48,40},{56,48},{64,56},{72,6... | collective-permute-start | bytes 1179656 | tf_op jit(solution)/shard_map/ppermute | solution.py:31
  799.1 82.5 %collective-permute-start.12 = (f32[1,4,4,2,3,16,128]{6,5,1,3,0,4,2:T(8,128)S(1)}, f32[1,4,4,2,3,16,128]{6,5,1,3,0,4,2:T(8,128)S(1)}, u32[]{:S(2)}, u32[]{:S(2)}) collective-permute-start(f32[1,4,4,2,3,16,128]{6,5,1,3,0,4,2:T(8,128)S(1)} %get-tuple-element.180), channel_id=1, source_target_pairs={{0,1},{1,2},{2,3},{3,4},{4,5},{5,6},{6,7},{7,0},{8,9},{9,10},{10,1... | collective-permute-start | bytes 2359304 | tf_op jit(solution)/shard_map/ppermute | solution.py:29
  864.3 23.8 %collective-permute-start.13 = (f32[1,4,4,2,3,16,128]{6,5,1,3,0,4,2:T(8,128)S(1)}, f32[1,4,4,2,3,16,128]{6,5,1,3,0,4,2:T(8,128)S(1)}, u32[]{:S(2)}, u32[]{:S(2)}) collective-permute-start(f32[1,4,4,2,3,16,128]{6,5,1,3,0,4,2:T(8,128)S(1)} %get-tuple-element.181), channel_id=1, source_target_pairs={{1,0},{2,1},{3,2},{4,3},{5,4},{6,5},{7,6},{0,7},{9,8},{10,9},{11,1... | collective-permute-start | bytes 2359304 | tf_op jit(solution)/shard_map/ppermute | solution.py:31
  897.3 19.9 %collective-permute-start.14 = (f32[2,1,4,2,3,16,128]{6,5,1,3,2,0,4:T(8,128)S(1)}, f32[2,1,4,2,3,16,128]{6,5,1,3,2,0,4:T(8,128)S(1)}, u32[]{:S(2)}, u32[]{:S(2)}) collective-permute-start(f32[2,1,4,2,3,16,128]{6,5,1,3,2,0,4:T(8,128)S(1)} %get-tuple-element.211), channel_id=1, source_target_pairs={{0,8},{8,16},{16,24},{24,32},{32,40},{40,48},{48,56},{56,64},{64,7... | collective-permute-start | bytes 1179656 | tf_op jit(solution)/shard_map/ppermute | solution.py:29
  899.2 18.0 %collective-permute-start.15 = (f32[2,1,4,2,3,16,128]{6,5,1,3,2,0,4:T(8,128)S(1)}, f32[2,1,4,2,3,16,128]{6,5,1,3,2,0,4:T(8,128)S(1)}, u32[]{:S(2)}, u32[]{:S(2)}) collective-permute-start(f32[2,1,4,2,3,16,128]{6,5,1,3,2,0,4:T(8,128)S(1)} %get-tuple-element.212), channel_id=1, source_target_pairs={{8,0},{16,8},{24,16},{32,24},{40,32},{48,40},{56,48},{64,56},{72,6... | collective-permute-start | bytes 1179656 | tf_op jit(solution)/shard_map/ppermute | solution.py:31
  917.5 20.6 %collective-permute-start.16 = (f32[1,4,4,2,3,16,128]{6,5,1,3,2,0,4:T(8,128)S(1)}, f32[1,4,4,2,3,16,128]{6,5,1,3,2,0,4:T(8,128)S(1)}, u32[]{:S(2)}, u32[]{:S(2)}) collective-permute-start(f32[1,4,4,2,3,16,128]{6,5,1,3,2,0,4:T(8,128)S(1)} %get-tuple-element.178), channel_id=1, source_target_pairs={{0,1},{1,2},{2,3},{3,4},{4,5},{5,6},{6,7},{7,0},{8,9},{9,10},{10,1... | collective-permute-start | bytes 2359304 | tf_op jit(solution)/shard_map/ppermute | solution.py:29
  925.0 22.6 %collective-permute-start.17 = (f32[1,4,4,2,3,16,128]{6,5,1,3,2,0,4:T(8,128)S(1)}, f32[1,4,4,2,3,16,128]{6,5,1,3,2,0,4:T(8,128)S(1)}, u32[]{:S(2)}, u32[]{:S(2)}) collective-permute-start(f32[1,4,4,2,3,16,128]{6,5,1,3,2,0,4:T(8,128)S(1)} %get-tuple-element.179), channel_id=1, source_target_pairs={{1,0},{2,1},{3,2},{4,3},{5,4},{6,5},{7,6},{0,7},{9,8},{10,9},{11,1... | collective-permute-start | bytes 2359304 | tf_op jit(solution)/shard_map/ppermute | solution.py:31
  (83 other events, 286.6 us)
Sparse Core Ops, SparseCore 0:
  125.2 530.6 all-reduce.2
where the time goes:
time: 964 us; the launch traced here: 963 us
  waiting for transfers between devices  629 us (65%)
  starting transfers between devices  140 us (15%)
  blocking collectives  125 us (13%)
  other arithmetic  30.5 us (3%)
  between operations  18.4 us (2%)
  local copies, waits for them, and re-layouts  16.3 us (2%)
    unnamed x2, waiting for transfers between devices  531 us
    all_gather x1, blocking collectives, on_device(): lax.all_gather(mix_coefficients(elemental, share_sums), 'space', axis=2,...  125 us
    ppermute x8, starting transfers between devices, extended(): lax.ppermute(tail, axis, [(i, (i + 1) % count) for i in range(count)])  89 us
    ppermute x8, waiting for transfers between devices, extended(): lax.ppermute(tail, axis, [(i, (i + 1) % count) for i in range(count)])  64.6 us
    ppermute x8, starting transfers between devices, extended(): lax.ppermute(head, axis, [((i + 1) % count, i) for i in range(count)])  42.4 us
    ppermute x8, waiting for transfers between devices, extended(): lax.ppermute(head, axis, [((i + 1) % count, i) for i in range(count)])  34 us
  transfers between devices with their start and end apart: 19, of which 14 were waited for; matrix products, arithmetic and copies ran while one was open for 1% of the time, Pallas kernels for 0%

commit v1 on v0

--- a/solution.py
+++ b/solution.py
@@ -229,8 +229,14 @@
         * normaliser
     )
     share_sums = lax.psum_scatter(partial_sums, "space", scatter_dimension=2, tiled=True)
-    mixed_coef = lax.all_gather(
-        mix_coefficients(elemental, share_sums), "space", axis=2, tiled=True
+    mixed_coef = jnp.concatenate(
+        lax.all_to_all(
+            jnp.stack([mix_coefficients(elemental, share_sums)] * lax.axis_size("space")),
+            "space",
+            0,
+            0,
+        ),
+        axis=2,
     )
     complex_pairs = mixed_coef.reshape(slices, eigen_count, 4, column_list, 2)
     mixed_real = complex_pairs[..., 0]

time: 964 us -> 819 us (0.85)
  the two profiles are of different devices: /device:TPU:129 before, /device:TPU:191 now
where the time goes in v1:
time: 819 us; the launch traced here: 818 us
  waiting for transfers between devices  649 us (79%)
  starting transfers between devices  107 us (13%)
  other arithmetic  27.8 us (3%)
  between operations  18 us (2%)
  local copies, waits for them, and re-layouts  13.2 us (2%)
    unnamed x2, waiting for transfers between devices  528 us
    ppermute x8, waiting for transfers between devices, extended(): lax.ppermute(tail, axis, [(i, (i + 1) % count) for i in range(count)])  68.8 us
    ppermute x8, starting transfers between devices, extended(): lax.ppermute(tail, axis, [(i, (i + 1) % count) for i in range(count)])  65.2 us
    ppermute x8, waiting for transfers between devices, extended(): lax.ppermute(head, axis, [((i + 1) % count, i) for i in range(count)])  45.8 us
    ppermute x8, starting transfers between devices, extended(): lax.ppermute(head, axis, [((i + 1) % count, i) for i in range(count)])  19.3 us
  transfers between devices with their start and end apart: 20, of which 16 were waited for; matrix products, arithmetic and copies ran while one was open for 1% of the time, Pallas kernels for 0%

profile of v1, /device:TPU:191, one launch (start us, length us, event | category | flops | bytes accessed | tf_op | source)
XLA Modules:
  0.0 818.2 jit_solution(7010871602118955236)
XLA Ops:
  6.5 1.1 copy_convert_fusion
  7.8 3.1 collective-permute-start
  10.9 2.2 collective-permute-start.1
  13.1 0.7 fusion.201
  13.8 8.1 collective-permute-start.5
  22.0 0.7 slice_bitcast_fusion.381
  22.8 6.4 collective-permute-start.4
  29.2 0.9 copy_convert_fusion.1
  31.8 3.0 collective-permute-start.2
  34.8 1.9 collective-permute-start.3
  37.0 15.0 %collective-permute-done.2 = f32[1,4,4,2,3,16,128]{6,5,1,3,0,4,2:T(8,128)S(1)} collective-permute-done((f32[1,4,4,2,3,16,128]{6,5,1,3,0,4,2:T(8,128)S(1)}, f32[1,4,4,2,3,16,128]{6,5,1,3,0,4,2:T(8,128)S(1)}, u32[]{:S(2)}, u32[]{:S(2)}) %collective-permute-start.2) | collective-permute-done | bytes 786464 | tf_op jit(solution)/shard_map/ppermute | solution.py:29
  52.0 6.3 collective-permute-done.3
  58.3 0.6 maximum_multiply_fusion
  66.2 1.9 collective-permute-start.6
  68.2 3.5 collective-permute-start.7
  71.7 3.9 collective-permute-done.6
  75.5 6.0 collective-permute-done.7
  81.8 5.7 collective-permute-start.8
  87.5 2.1 collective-permute-start.9
  89.8 15.0 %collective-permute-done.8 = f32[1,4,4,2,3,16,128]{6,5,1,3,0,4,2:T(8,128)S(1)} collective-permute-done((f32[1,4,4,2,3,16,128]{6,5,1,3,0,4,2:T(8,128)S(1)}, f32[1,4,4,2,3,16,128]{6,5,1,3,0,4,2:T(8,128)S(1)}, u32[]{:S(2)}, u32[]{:S(2)}) %collective-permute-start.8) | collective-permute-done | bytes 786464 | tf_op jit(solution)/shard_map/ppermute | solution.py:29
  104.8 4.9 collective-permute-done.9
  109.7 0.6 maximum_multiply_fusion.1
  119.0 0.9 copy.792
  119.9 1.3 dynamic-slice
  121.8 528.1 %all-reduce.3.cloned.1.call-done = f32[2,256,128]{1,0,2:T(2,128)} async-done(((f32[2,256,128]{1,0,2:T(2,128)}), f32[2,256,128]{1,0,2:T(2,128)}) %all-reduce.3.cloned.1.call-update) | async-done | bytes 262160
  649.9 0.7 dynamic-slice_bitcast_fusion
  651.9 0.7 stack.619
  652.6 8.0 all-to-all-start
  660.7 6.5 all-to-all-done
  668.2 6.2 collective-permute-start.10
  674.5 1.9 collective-permute-start.11
  676.4 2.8 collective-permute-done.10
  679.1 8.1 collective-permute-done.11
  687.5 37.1 %collective-permute-start.12 = (f32[1,4,4,2,3,16,128]{6,5,1,3,0,4,2:T(8,128)S(1)}, f32[1,4,4,2,3,16,128]{6,5,1,3,0,4,2:T(8,128)S(1)}, u32[]{:S(2)}, u32[]{:S(2)}) collective-permute-start(f32[1,4,4,2,3,16,128]{6,5,1,3,0,4,2:T(8,128)S(1)} %get-tuple-element.180), channel_id=1, source_target_pairs={{0,1},{1,2},{2,3},{3,4},{4,5},{5,6},{6,7},{7,0},{8,9},{9,10},{10,1... | collective-permute-start | bytes 2359304 | tf_op jit(solution)/shard_map/ppermute | solution.py:29
  724.7 2.1 collective-permute-start.13
  726.8 13.9 %collective-permute-done.12 = f32[1,4,4,2,3,16,128]{6,5,1,3,0,4,2:T(8,128)S(1)} collective-permute-done((f32[1,4,4,2,3,16,128]{6,5,1,3,0,4,2:T(8,128)S(1)}, f32[1,4,4,2,3,16,128]{6,5,1,3,0,4,2:T(8,128)S(1)}, u32[]{:S(2)}, u32[]{:S(2)}) %collective-permute-start.12) | collective-permute-done | bytes 786464 | tf_op jit(solution)/shard_map/ppermute | solution.py:29
  740.7 7.8 collective-permute-done.13
  748.5 0.6 maximum_multiply_fusion.2
  757.0 0.6 fusion.12
  757.6 1.9 collective-permute-start.14
  759.6 3.4 collective-permute-start.15
  762.9 3.5 collective-permute-done.14
  766.4 5.9 collective-permute-done.15
  772.6 6.2 collective-permute-start.16
  778.9 2.2 collective-permute-start.17
  781.1 14.8 %collective-permute-done.16 = f32[1,4,4,2,3,16,128]{6,5,1,3,2,0,4:T(8,128)S(1)} collective-permute-done((f32[1,4,4,2,3,16,128]{6,5,1,3,2,0,4:T(8,128)S(1)}, f32[1,4,4,2,3,16,128]{6,5,1,3,2,0,4:T(8,128)S(1)}, u32[]{:S(2)}, u32[]{:S(2)}) %collective-permute-start.16) | collective-permute-done | bytes 786464 | tf_op jit(solution)/shard_map/ppermute | solution.py:29
  795.8 6.8 collective-permute-done.17
  810.5 0.8 copy.858
  (551 shorter events, 33.5 us)
Async XLA Ops:
  6.5 643.4 %all-reduce.3.cloned.1.call-start = ((), (), s32[]{:S(2)}) async-start(), calls=%async_computation.1 | async-start | bytes 524288
  7.8 23.7 %collective-permute-start = (f32[2,1,4,2,3,16,128]{6,5,1,3,0,4,2:T(8,128)S(1)}, f32[2,1,4,2,3,16,128]{6,5,1,3,0,4,2:T(8,128)S(1)}, u32[]{:S(2)}, u32[]{:S(2)}) collective-permute-start(f32[2,1,4,2,3,16,128]{6,5,1,3,0,4,2:T(8,128)S(1)} %get-tuple-element.247), channel_id=1, source_target_pairs={{0,8},{8,16},{16,24},{24,32},{32,40},{40,48},{48,56},{56,64},{64,7... | collective-permute-start | bytes 1179656 | tf_op jit(solution)/shard_map/ppermute | solution.py:29
  10.9 20.6 %collective-permute-start.1 = (f32[2,1,4,2,3,16,128]{6,5,1,3,0,4,2:T(8,128)S(1)}, f32[2,1,4,2,3,16,128]{6,5,1,3,0,4,2:T(8,128)S(1)}, u32[]{:S(2)}, u32[]{:S(2)}) collective-permute-start(f32[2,1,4,2,3,16,128]{6,5,1,3,0,4,2:T(8,128)S(1)} %get-tuple-element.248), channel_id=1, source_target_pairs={{8,0},{16,8},{24,16},{32,24},{40,32},{48,40},{56,48},{64,56},{72,6... | collective-permute-start | bytes 1179656 | tf_op jit(solution)/shard_map/ppermute | solution.py:31
  13.8 17.6 %collective-permute-start.5 = (bf16[1,2,2,3,3,128]{5,1,4,3,2,0:T(2,128)(2,1)S(1)}, bf16[1,2,2,3,3,128]{5,1,4,3,2,0:T(2,128)(2,1)S(1)}, u32[]{:S(2)}, u32[]{:S(2)}) collective-permute-start(bf16[1,2,2,3,3,128]{5,1,4,3,2,0:T(2,128)(2,1)S(1)} %bitcast.1311), channel_id=1, source_target_pairs={{0,1},{1,2},{2,3},{3,4},{4,5},{5,6},{6,7},{7,0},{8,9},{9,10},{10,1... | collective-permute-start | bytes 27656 | tf_op jit(solution)/shard_map/ppermute | solution.py:19
  22.8 14.0 %collective-permute-start.4 = (bf16[2,1,2,3,3,128]{5,1,4,3,2,0:T(2,128)(2,1)S(1)}, bf16[2,1,2,3,3,128]{5,1,4,3,2,0:T(2,128)(2,1)S(1)}, u32[]{:S(2)}, u32[]{:S(2)}) collective-permute-start(bf16[2,1,2,3,3,128]{5,1,4,3,2,0:T(2,128)(2,1)S(1)} %copy.760), channel_id=1, source_target_pairs={{0,8},{8,16},{16,24},{24,32},{32,40},{40,48},{48,56},{56,64},{64,7... | collective-permute-start | bytes 27656 | tf_op jit(solution)/shard_map/ppermute | solution.py:19
  30.3 86.0 %copy-start.73 = (pred[128]{0:T(512)(128)(4,1)}, pred[128]{0:T(512)(128)(4,1)S(1)}, u32[]{:S(2)}) copy-start(pred[128]{0:T(512)(128)(4,1)S(1)} %broadcast_compare_fusion.1) | copy-start | bytes 388
  30.3 86.5 %copy-start.71 = (pred[128]{0:T(512)(128)(4,1)}, pred[128]{0:T(512)(128)(4,1)S(1)}, u32[]{:S(2)}) copy-start(pred[128]{0:T(512)(128)(4,1)S(1)} %broadcast_compare_fusion) | copy-start | bytes 388
  30.3 84.9 %copy-start.22 = (f32[2,2,3,128]{3,1,2,0:T(2,128)}, f32[2,2,3,128]{3,1,2,0:T(2,128)S(1)}, u32[]{:S(2)}) copy-start(f32[2,2,3,128]{3,1,2,0:T(2,128)S(1)} %get-tuple-element.761) | copy-start | bytes 18436
  30.3 84.9 %copy-start.24 = (f32[2,2,3,128]{3,1,2,0:T(2,128)}, f32[2,2,3,128]{3,1,2,0:T(2,128)S(1)}, u32[]{:S(2)}) copy-start(f32[2,2,3,128]{3,1,2,0:T(2,128)S(1)} %get-tuple-element.762) | copy-start | bytes 18436
  30.4 84.9 %copy-start.26 = (f32[2,2,3,128]{3,1,2,0:T(2,128)}, f32[2,2,3,128]{3,1,2,0:T(2,128)S(1)}, u32[]{:S(2)}) copy-start(f32[2,2,3,128]{3,1,2,0:T(2,128)S(1)} %get-tuple-element.763) | copy-start | bytes 18436
  30.4 84.9 %copy-start.28 = (f32[2,2,3,128]{3,1,2,0:T(2,128)}, f32[2,2,3,128]{3,1,2,0:T(2,128)S(1)}, u32[]{:S(2)}) copy-start(f32[2,2,3,128]{3,1,2,0:T(2,128)S(1)} %get-tuple-element.764) | copy-start | bytes 18436
  30.4 84.9 %copy-start.30 = (f32[2,2,3,128]{3,1,2,0:T(2,128)}, f32[2,2,3,128]{3,1,2,0:T(2,128)S(1)}, u32[]{:S(2)}) copy-start(f32[2,2,3,128]{3,1,2,0:T(2,128)S(1)} %get-tuple-element.765) | copy-start | bytes 18436
  30.4 84.9 %copy-start.32 = (f32[2,2,3,128]{3,1,2,0:T(2,128)}, f32[2,2,3,128]{3,1,2,0:T(2,128)S(1)}, u32[]{:S(2)}) copy-start(f32[2,2,3,128]{3,1,2,0:T(2,128)S(1)} %get-tuple-element.766) | copy-start | bytes 18436
  30.4 82.1 %copy-start.46 = (f32[2,2,3,128]{3,1,2,0:T(2,128)}, f32[2,2,3,128]{3,1,2,0:T(2,128)S(1)}, u32[]{:S(2)}) copy-start(f32[2,2,3,128]{3,1,2,0:T(2,128)S(1)} %get-tuple-element.767) | copy-start | bytes 18436
  30.4 82.1 %copy-start.48 = (f32[2,2,3,128]{3,1,2,0:T(2,128)}, f32[2,2,3,128]{3,1,2,0:T(2,128)S(1)}, u32[]{:S(2)}) copy-start(f32[2,2,3,128]{3,1,2,0:T(2,128)S(1)} %get-tuple-element.768) | copy-start | bytes 18436
  30.4 82.1 %copy-start.50 = (f32[2,2,3,128]{3,1,2,0:T(2,128)}, f32[2,2,3,128]{3,1,2,0:T(2,128)S(1)}, u32[]{:S(2)}) copy-start(f32[2,2,3,128]{3,1,2,0:T(2,128)S(1)} %get-tuple-element.769) | copy-start | bytes 18436
  30.5 82.1 %copy-start.52 = (f32[2,2,3,128]{3,1,2,0:T(2,128)}, f32[2,2,3,128]{3,1,2,0:T(2,128)S(1)}, u32[]{:S(2)}) copy-start(f32[2,2,3,128]{3,1,2,0:T(2,128)S(1)} %get-tuple-element.770) | copy-start | bytes 18436
  30.5 82.1 %copy-start.54 = (f32[2,2,3,128]{3,1,2,0:T(2,128)}, f32[2,2,3,128]{3,1,2,0:T(2,128)S(1)}, u32[]{:S(2)}) copy-start(f32[2,2,3,128]{3,1,2,0:T(2,128)S(1)} %get-tuple-element.771) | copy-start | bytes 18436
  30.5 82.1 %copy-start.56 = (f32[2,2,3,128]{3,1,2,0:T(2,128)}, f32[2,2,3,128]{3,1,2,0:T(2,128)S(1)}, u32[]{:S(2)}) copy-start(f32[2,2,3,128]{3,1,2,0:T(2,128)S(1)} %get-tuple-element.772) | copy-start | bytes 18436
  31.3 82.3 %copy-start.10 = (f32[2,2,3,128]{3,1,2,0:T(2,128)}, f32[2,2,3,128]{3,1,2,0:T(2,128)S(1)}, u32[]{:S(2)}) copy-start(f32[2,2,3,128]{3,1,2,0:T(2,128)S(1)} %get-tuple-element.717) | copy-start | bytes 18436
  31.3 82.3 %copy-start.12 = (f32[2,2,3,128]{3,1,2,0:T(2,128)}, f32[2,2,3,128]{3,1,2,0:T(2,128)S(1)}, u32[]{:S(2)}) copy-start(f32[2,2,3,128]{3,1,2,0:T(2,128)S(1)} %get-tuple-element.718) | copy-start | bytes 18436
  31.3 82.3 %copy-start.14 = (f32[2,2,3,128]{3,1,2,0:T(2,128)}, f32[2,2,3,128]{3,1,2,0:T(2,128)S(1)}, u32[]{:S(2)}) copy-start(f32[2,2,3,128]{3,1,2,0:T(2,128)S(1)} %get-tuple-element.719) | copy-start | bytes 18436
  31.3 82.3 %copy-start.16 = (f32[2,2,3,128]{3,1,2,0:T(2,128)}, f32[2,2,3,128]{3,1,2,0:T(2,128)S(1)}, u32[]{:S(2)}) copy-start(f32[2,2,3,128]{3,1,2,0:T(2,128)S(1)} %get-tuple-element.720) | copy-start | bytes 18436
  31.3 82.3 %copy-start.18 = (f32[2,2,3,128]{3,1,2,0:T(2,128)}, f32[2,2,3,128]{3,1,2,0:T(2,128)S(1)}, u32[]{:S(2)}) copy-start(f32[2,2,3,128]{3,1,2,0:T(2,128)S(1)} %get-tuple-element.721) | copy-start | bytes 18436
  31.3 82.3 %copy-start.20 = (f32[2,2,3,128]{3,1,2,0:T(2,128)}, f32[2,2,3,128]{3,1,2,0:T(2,128)S(1)}, u32[]{:S(2)}) copy-start(f32[2,2,3,128]{3,1,2,0:T(2,128)S(1)} %get-tuple-element.722) | copy-start | bytes 18436
  31.3 82.9 %copy-start.2 = (f32[2,2,3,128]{3,1,2,0:T(2,128)}, f32[2,2,3,128]{3,1,2,0:T(2,128)S(1)}, u32[]{:S(2)}) copy-start(f32[2,2,3,128]{3,1,2,0:T(2,128)S(1)} %get-tuple-element.795) | copy-start | bytes 18436
  31.3 82.9 %copy-start.4 = (f32[2,2,3,128]{3,1,2,0:T(2,128)}, f32[2,2,3,128]{3,1,2,0:T(2,128)S(1)}, u32[]{:S(2)}) copy-start(f32[2,2,3,128]{3,1,2,0:T(2,128)S(1)} %get-tuple-element.796) | copy-start | bytes 18436
  31.4 82.9 %copy-start.6 = (f32[2,2,3,128]{3,1,2,0:T(2,128)}, f32[2,2,3,128]{3,1,2,0:T(2,128)S(1)}, u32[]{:S(2)}) copy-start(f32[2,2,3,128]{3,1,2,0:T(2,128)S(1)} %get-tuple-element.797) | copy-start | bytes 18436
  31.4 82.9 %copy-start.8 = (f32[2,2,3,128]{3,1,2,0:T(2,128)}, f32[2,2,3,128]{3,1,2,0:T(2,128)S(1)}, u32[]{:S(2)}) copy-start(f32[2,2,3,128]{3,1,2,0:T(2,128)S(1)} %get-tuple-element.798) | copy-start | bytes 18436
  31.4 78.3 %copy-start.75 = (f32[4]{0:T(128)}, f32[4]{0:T(128)S(1)}, u32[]{:S(2)}) copy-start(f32[4]{0:T(128)S(1)} %or_select_fusion) | copy-start | bytes 52
  31.8 20.2 %collective-permute-start.2 = (f32[1,4,4,2,3,16,128]{6,5,1,3,0,4,2:T(8,128)S(1)}, f32[1,4,4,2,3,16,128]{6,5,1,3,0,4,2:T(8,128)S(1)}, u32[]{:S(2)}, u32[]{:S(2)}) collective-permute-start(f32[1,4,4,2,3,16,128]{6,5,1,3,0,4,2:T(8,128)S(1)} %get-tuple-element.187), channel_id=1, source_target_pairs={{0,1},{1,2},{2,3},{3,4},{4,5},{5,6},{6,7},{7,0},{8,9},{9,10},{10,1... | collective-permute-start | bytes 2359304 | tf_op jit(solution)/shard_map/ppermute | solution.py:29
  34.8 23.5 %collective-permute-start.3 = (f32[1,4,4,2,3,16,128]{6,5,1,3,0,4,2:T(8,128)S(1)}, f32[1,4,4,2,3,16,128]{6,5,1,3,0,4,2:T(8,128)S(1)}, u32[]{:S(2)}, u32[]{:S(2)}) collective-permute-start(f32[1,4,4,2,3,16,128]{6,5,1,3,0,4,2:T(8,128)S(1)} %get-tuple-element.188), channel_id=1, source_target_pairs={{1,0},{2,1},{3,2},{4,3},{5,4},{6,5},{7,6},{0,7},{9,8},{10,9},{11,1... | collective-permute-start | bytes 2359304 | tf_op jit(solution)/shard_map/ppermute | solution.py:31
  36.9 77.6 %copy-start.34 = (f32[2,2,3,128]{3,1,2,0:T(2,128)}, f32[2,2,3,128]{3,1,2,0:T(2,128)S(1)}, u32[]{:S(2)}) copy-start(f32[2,2,3,128]{3,1,2,0:T(2,128)S(1)} %get-tuple-element.758) | copy-start | bytes 18436
  36.9 77.6 %copy-start.36 = (f32[2,2,3,128]{3,1,2,0:T(2,128)}, f32[2,2,3,128]{3,1,2,0:T(2,128)S(1)}, u32[]{:S(2)}) copy-start(f32[2,2,3,128]{3,1,2,0:T(2,128)S(1)} %get-tuple-element.759) | copy-start | bytes 18436
  66.2 9.3 %collective-permute-start.6 = (f32[2,1,4,2,3,16,128]{6,5,1,3,0,4,2:T(8,128)S(1)}, f32[2,1,4,2,3,16,128]{6,5,1,3,0,4,2:T(8,128)S(1)}, u32[]{:S(2)}, u32[]{:S(2)}) collective-permute-start(f32[2,1,4,2,3,16,128]{6,5,1,3,0,4,2:T(8,128)S(1)} %get-tuple-element.235), channel_id=1, source_target_pairs={{0,8},{8,16},{16,24},{24,32},{32,40},{40,48},{48,56},{56,64},{64,7... | collective-permute-start | bytes 1179656 | tf_op jit(solution)/shard_map/ppermute | solution.py:29
  68.2 13.4 %collective-permute-start.7 = (f32[2,1,4,2,3,16,128]{6,5,1,3,0,4,2:T(8,128)S(1)}, f32[2,1,4,2,3,16,128]{6,5,1,3,0,4,2:T(8,128)S(1)}, u32[]{:S(2)}, u32[]{:S(2)}) collective-permute-start(f32[2,1,4,2,3,16,128]{6,5,1,3,0,4,2:T(8,128)S(1)} %get-tuple-element.236), channel_id=1, source_target_pairs={{8,0},{16,8},{24,16},{32,24},{40,32},{48,40},{56,48},{64,56},{72,6... | collective-permute-start | bytes 1179656 | tf_op jit(solution)/shard_map/ppermute | solution.py:31
  81.8 23.0 %collective-permute-start.8 = (f32[1,4,4,2,3,16,128]{6,5,1,3,0,4,2:T(8,128)S(1)}, f32[1,4,4,2,3,16,128]{6,5,1,3,0,4,2:T(8,128)S(1)}, u32[]{:S(2)}, u32[]{:S(2)}) collective-permute-start(f32[1,4,4,2,3,16,128]{6,5,1,3,0,4,2:T(8,128)S(1)} %get-tuple-element.185), channel_id=1, source_target_pairs={{0,1},{1,2},{2,3},{3,4},{4,5},{5,6},{6,7},{7,0},{8,9},{9,10},{10,1... | collective-permute-start | bytes 2359304 | tf_op jit(solution)/shard_map/ppermute | solution.py:29
  87.5 22.2 %collective-permute-start.9 = (f32[1,4,4,2,3,16,128]{6,5,1,3,0,4,2:T(8,128)S(1)}, f32[1,4,4,2,3,16,128]{6,5,1,3,0,4,2:T(8,128)S(1)}, u32[]{:S(2)}, u32[]{:S(2)}) collective-permute-start(f32[1,4,4,2,3,16,128]{6,5,1,3,0,4,2:T(8,128)S(1)} %get-tuple-element.186), channel_id=1, source_target_pairs={{1,0},{2,1},{3,2},{4,3},{5,4},{6,5},{7,6},{0,7},{9,8},{10,9},{11,1... | collective-permute-start | bytes 2359304 | tf_op jit(solution)/shard_map/ppermute | solution.py:31
  117.9 532.7 %copy-start = (bf16[2,2,256,256]{3,2,1,0:T(8,128)(2,1)S(1)}, bf16[2,2,256,256]{3,2,1,0:T(8,128)(2,1)}, u32[]{:S(2)}) copy-start(bf16[2,2,256,256]{3,2,1,0:T(8,128)(2,1)} %param.9) | copy-start | bytes 1572868
  652.6 14.7 %all-to-all-start = ((bf16[64,2,256,2]{2,1,3,0:T(2,128)(2,1)}), bf16[64,2,256,2]{2,1,3,0:T(2,128)(2,1)S(1)}, u32[]{:S(2)}, u32[]{:S(2)}) async-start(bf16[64,2,256,2]{2,1,3,0:T(2,128)(2,1)} %stack.619), calls=%async_computation | async-start | bytes 262144 | tf_op jit(solution)/shard_map/all_to_all | solution.py:233
  668.2 10.9 %collective-permute-start.10 = (f32[2,1,4,2,3,16,128]{6,5,1,3,0,4,2:T(8,128)S(1)}, f32[2,1,4,2,3,16,128]{6,5,1,3,0,4,2:T(8,128)S(1)}, u32[]{:S(2)}, u32[]{:S(2)}) collective-permute-start(f32[2,1,4,2,3,16,128]{6,5,1,3,0,4,2:T(8,128)S(1)} %get-tuple-element.223), channel_id=1, source_target_pairs={{0,8},{8,16},{16,24},{24,32},{32,40},{40,48},{48,56},{56,64},{64,7... | collective-permute-start | bytes 1179656 | tf_op jit(solution)/shard_map/ppermute | solution.py:29
  674.5 12.7 %collective-permute-start.11 = (f32[2,1,4,2,3,16,128]{6,5,1,3,0,4,2:T(8,128)S(1)}, f32[2,1,4,2,3,16,128]{6,5,1,3,0,4,2:T(8,128)S(1)}, u32[]{:S(2)}, u32[]{:S(2)}) collective-permute-start(f32[2,1,4,2,3,16,128]{6,5,1,3,0,4,2:T(8,128)S(1)} %get-tuple-element.224), channel_id=1, source_target_pairs={{8,0},{16,8},{24,16},{32,24},{40,32},{48,40},{56,48},{64,56},{72,6... | collective-permute-start | bytes 1179656 | tf_op jit(solution)/shard_map/ppermute | solution.py:31
  687.5 53.2 %collective-permute-start.12 = (f32[1,4,4,2,3,16,128]{6,5,1,3,0,4,2:T(8,128)S(1)}, f32[1,4,4,2,3,16,128]{6,5,1,3,0,4,2:T(8,128)S(1)}, u32[]{:S(2)}, u32[]{:S(2)}) collective-permute-start(f32[1,4,4,2,3,16,128]{6,5,1,3,0,4,2:T(8,128)S(1)} %get-tuple-element.180), channel_id=1, source_target_pairs={{0,1},{1,2},{2,3},{3,4},{4,5},{5,6},{6,7},{7,0},{8,9},{9,10},{10,1... | collective-permute-start | bytes 2359304 | tf_op jit(solution)/shard_map/ppermute | solution.py:29
  724.7 23.8 %collective-permute-start.13 = (f32[1,4,4,2,3,16,128]{6,5,1,3,0,4,2:T(8,128)S(1)}, f32[1,4,4,2,3,16,128]{6,5,1,3,0,4,2:T(8,128)S(1)}, u32[]{:S(2)}, u32[]{:S(2)}) collective-permute-start(f32[1,4,4,2,3,16,128]{6,5,1,3,0,4,2:T(8,128)S(1)} %get-tuple-element.181), channel_id=1, source_target_pairs={{1,0},{2,1},{3,2},{4,3},{5,4},{6,5},{7,6},{0,7},{9,8},{10,9},{11,1... | collective-permute-start | bytes 2359304 | tf_op jit(solution)/shard_map/ppermute | solution.py:31
  757.6 8.8 %collective-permute-start.14 = (f32[2,1,4,2,3,16,128]{6,5,1,3,2,0,4:T(8,128)S(1)}, f32[2,1,4,2,3,16,128]{6,5,1,3,2,0,4:T(8,128)S(1)}, u32[]{:S(2)}, u32[]{:S(2)}) collective-permute-start(f32[2,1,4,2,3,16,128]{6,5,1,3,2,0,4:T(8,128)S(1)} %get-tuple-element.211), channel_id=1, source_target_pairs={{0,8},{8,16},{16,24},{24,32},{32,40},{40,48},{48,56},{56,64},{64,7... | collective-permute-start | bytes 1179656 | tf_op jit(solution)/shard_map/ppermute | solution.py:29
  759.6 12.7 %collective-permute-start.15 = (f32[2,1,4,2,3,16,128]{6,5,1,3,2,0,4:T(8,128)S(1)}, f32[2,1,4,2,3,16,128]{6,5,1,3,2,0,4:T(8,128)S(1)}, u32[]{:S(2)}, u32[]{:S(2)}) collective-permute-start(f32[2,1,4,2,3,16,128]{6,5,1,3,2,0,4:T(8,128)S(1)} %get-tuple-element.212), channel_id=1, source_target_pairs={{8,0},{16,8},{24,16},{32,24},{40,32},{48,40},{56,48},{64,56},{72,6... | collective-permute-start | bytes 1179656 | tf_op jit(solution)/shard_map/ppermute | solution.py:31
  772.6 23.2 %collective-permute-start.16 = (f32[1,4,4,2,3,16,128]{6,5,1,3,2,0,4:T(8,128)S(1)}, f32[1,4,4,2,3,16,128]{6,5,1,3,2,0,4:T(8,128)S(1)}, u32[]{:S(2)}, u32[]{:S(2)}) collective-permute-start(f32[1,4,4,2,3,16,128]{6,5,1,3,2,0,4:T(8,128)S(1)} %get-tuple-element.178), channel_id=1, source_target_pairs={{0,1},{1,2},{2,3},{3,4},{4,5},{5,6},{6,7},{7,0},{8,9},{9,10},{10,1... | collective-permute-start | bytes 2359304 | tf_op jit(solution)/shard_map/ppermute | solution.py:29
  778.9 23.8 %collective-permute-start.17 = (f32[1,4,4,2,3,16,128]{6,5,1,3,2,0,4:T(8,128)S(1)}, f32[1,4,4,2,3,16,128]{6,5,1,3,2,0,4:T(8,128)S(1)}, u32[]{:S(2)}, u32[]{:S(2)}) collective-permute-start(f32[1,4,4,2,3,16,128]{6,5,1,3,2,0,4:T(8,128)S(1)} %get-tuple-element.179), channel_id=1, source_target_pairs={{1,0},{2,1},{3,2},{4,3},{5,4},{6,5},{7,6},{0,7},{9,8},{10,9},{11,1... | collective-permute-start | bytes 2359304 | tf_op jit(solution)/shard_map/ppermute | solution.py:31
  (49 other events, 924.5 us)
Sparse Core Ops, SparseCore 0:
  120.0 529.8 all-reduce.2
